TPU v7x, 32 devices: a whole 2x2x4 slice. The times are simulated.
32 devices in a mesh: prow: 8 (over z, core), pcol: 4 (over y, x).
Axes of the slice: x: 2, y: 2, z: 4, core: 2. Of those that a mesh axis runs over, the one named last changes fastest.
Arguments:
- right_side: float32 [1024, 4, 4, 1024], P('prow', None, 'pcol'), may hold values from -6 to 6
- inverse_blocks: bfloat16 [2, 1, 8, 1024, 2, 4, 1024], P(None, None, 'prow', None, None, 'pcol'), as said below
- coupling: bfloat16 [1, 8, 1024, 2, 4, 1024], P(None, 'prow', None, None, 'pcol'), may hold values from -0.03125 to 0.03125
- pivots: int32 [2, 8, 1024], P(None, 'prow'), may hold values from 0 to 16383, as said below
Outputs:
- solution: bfloat16 [1024, 2, 8, 1024], P('pcol', None, 'prow')
Inputs may be any that keep to these rules, and one draw needn't show every extreme that they name: `inverse_blocks`: each block is unit upper triangular: ones on its diagonal, zeros below it. Every row number of the window appears exactly once; for every p and p2, exactly 16 * 1024 / 8 ** 2 of the entries pivots[:, p, :] are rows g with (g // 1024) % 8 == p2.
All inputs are finite; a program needn't handle non-finite values.
Results may differ from a plain program's by a relative error of at most 0.0052.
Values may be sent and summed in bfloat16 or wider, within the bound.
A program may use at most 128 MiB of HBM per device.

v0:
```python
import jax
import jax.numpy as jnp
from jax import lax
from jax.sharding import PartitionSpec as P


def body(right_side, inverse_blocks, coupling, pivots):
    bf16 = jnp.bfloat16
    f32 = jnp.float32
    rhs_here = right_side.shape[0]
    tiles_across = right_side.shape[1]
    tile_width = right_side.shape[3]
    blocks_here = inverse_blocks.shape[1]
    count_rows = blocks_here * tile_width
    tiles_half = inverse_blocks.shape[4]
    count_cols = tiles_half * tile_width
    inverse_pair = inverse_blocks.reshape(2, count_rows, count_cols)
    coupling_mat = coupling.reshape(count_rows, count_cols)
    rows_axis = lax.axis_size("prow")
    cols_axis = lax.axis_size("pcol")
    own_cols = rhs_here * rows_axis // cols_axis
    contract_last = (((1,), (1,)), ((), ()))
    me = lax.axis_index("prow")
    lower_rhs = right_side[:, :tiles_half].reshape(rhs_here, count_cols)
    upper_rhs = right_side[:, tiles_half:].astype(bf16).reshape(rhs_here, count_cols)
    own_pivots = pivots.reshape(-1)
    width = own_pivots.shape[0]
    share = width // rows_axis
    all_pivots = lax.all_gather(own_pivots, "prow", axis=0)

    def owner_of(rows):
        return rows // tile_width % rows_axis

    def local_of(rows):
        return rows // (tile_width * rows_axis) * tile_width + rows % tile_width

    mine = owner_of(all_pivots) == me
    slot = jnp.where(mine, jnp.cumsum(mine.astype(jnp.int32), axis=1) - 1, -1)
    hits = slot[:, :, None] == lax.broadcasted_iota(jnp.int32, (1, 1, share), 2)
    picked = jnp.sum(jnp.where(hits, local_of(all_pivots)[:, :, None], 0), axis=1)
    owner = owner_of(own_pivots)
    same = owner[None, :] == lax.broadcasted_iota(jnp.int32, (rows_axis, 1), 0)
    rank = jnp.sum(jnp.where(same, jnp.cumsum(same.astype(jnp.int32), axis=1) - 1, 0), axis=0)
    code = owner * share + rank

    def solve_with(inverse_mat, portion):
        return lax.dot_general(portion, inverse_mat, contract_last, preferred_element_type=bf16)

    first_partial = solve_with(
        inverse_pair[1], lax.all_gather(upper_rhs, "prow", axis=0, tiled=True)
    )
    upper_solved = lax.psum_scatter(first_partial, "pcol", scatter_dimension=0, tiled=True)
    update_partial = jnp.dot(
        lax.all_gather(upper_solved, "pcol", axis=0, tiled=True),
        coupling_mat,
        preferred_element_type=bf16,
    )
    update = lax.psum_scatter(update_partial, "prow", scatter_dimension=0, tiled=True)
    lower_ready = (lower_rhs - update.astype(f32)).astype(bf16)
    second_partial = solve_with(
        inverse_pair[0], lax.all_gather(lower_ready, "prow", axis=0, tiled=True)
    )
    lower_solved = lax.psum_scatter(second_partial, "pcol", scatter_dimension=0, tiled=True)
    joined = jnp.concatenate([lower_solved, upper_solved], axis=1)
    choose = (picked.reshape(-1)[None, :] == lax.broadcasted_iota(jnp.int32, (width, 1), 0)).astype(
        bf16
    )
    chosen = jnp.dot(joined, choose, preferred_element_type=bf16)
    received = lax.all_to_all(
        chosen.reshape(own_cols, rows_axis, share), "prow", split_axis=1, concat_axis=1
    ).reshape(own_cols, width)
    place = (code[None, :] == lax.broadcasted_iota(jnp.int32, (width, 1), 0)).astype(bf16)
    permuted = jnp.dot(received, place, preferred_element_type=bf16)
    return permuted.reshape(own_cols, pivots.shape[0], 1, tile_width)


def solution(mesh):
    in_specs = (
        P("prow", None, "pcol", None),
        P(None, None, "prow", None, None, "pcol", None),
        P(None, "prow", None, None, "pcol", None),
        P(None, "prow", None),
    )
    out_specs = P("pcol", None, "prow", None)
    return jax.shard_map(body, mesh=mesh, in_specs=in_specs, out_specs=out_specs, check_vma=False)
```

profile of v0, /device:TPU:0, one launch (start us, length us, event | category | flops | bytes accessed | tf_op | source)
XLA Modules:
  0.0 343.2 jit_solution(7763216155621803395)
XLA Ops:
  6.5 4.5 %fusion.9 = bf16[128,2,1024]{2,1,0:T(2,128)(2,1)S(1)} fusion(f32[128,4,1,1024]{3,2,1,0:T(1,128)} %param.4), kind=kLoop, calls=%fused_computation.12 | loop fusion | bytes 1048576 | tf_op jit(solution)/shard_map/slice | solution.py:25
  11.0 0.9 copy.21
  12.0 8.0 %fusion.32 = (bf16[1,1,1,1024,2,1,1024]{6,4,5,3,2,1,0:T(2,128)(2,1)}, bf16[1,1,1,1024,2,1,1024]{6,4,5,3,2,1,0:T(2,128)(2,1)S(1)}) fusion(bf16[2,1,1,1024,2,1,1024]{6,4,5,3,2,1,0:T(2,128)(2,1)} %param.5), kind=kLoop, calls=%fused_computation.72 | loop fusion | bytes 16777216 | tf_op jit(solution)/shard_map/slice | solution.py:61
  20.0 3.4 copy.22
  23.4 38.3 %all-gather.5.cloned.1.call-done = bf16[1024,2048]{1,0:T(8,128)(2,1)} async-done(((bf16[128,2048]{1,0:T(8,128)(2,1)}), bf16[1024,2048]{1,0:T(8,128)(2,1)}) %all-gather.5.cloned.1.call-update) | async-done | bytes 4194320 | tf_op jit(solution)/shard_map/all_gather | solution.py:50
  61.7 9.4 %fusion.33 = bf16[1024,1024]{1,0:T(8,128)(2,1)} fusion(bf16[1024,2048]{1,0:T(8,128)(2,1)} %all-gather.5.cloned.1.call-done, bf16[1024,2048]{1,0:T(8,128)(2,1)} %bitcast.86), kind=kOutput, calls=%fused_computation.73 | convolution fusion | flops 4294967296 | bytes 10485760 | tf_op jit(solution)/shard_map/dot_general | solution.py:47
  71.2 34.1 %reduce-scatter.4.cloned.1.call-done = bf16[256,1024]{1,0:T(8,128)(2,1)} async-done(((bf16[1024,1024]{1,0:T(8,128)(2,1)}), bf16[256,1024]{1,0:T(8,128)(2,1)}) %reduce-scatter.4.cloned.1.call-update) | async-done | bytes 524304 | tf_op jit(solution)/shard_map/reduce_scatter | solution.py:52
  105.5 5.6 %copy.23 = bf16[128,8,2,1024]{3,1,2,0:T(8,128)(2,1)} copy(bf16[128,8,2,1024]{3,2,1,0:T(2,128)(2,1)} %bitcast.85) | data formatting | bytes 8388608
  111.1 31.2 %all-gather.7.cloned.1.call-done = bf16[1024,1024]{1,0:T(8,128)(2,1)} async-done(((bf16[256,1024]{1,0:T(8,128)(2,1)}), bf16[1024,1024]{1,0:T(8,128)(2,1)}) %all-gather.7.cloned.1.call-update) | async-done | bytes 2097168 | tf_op jit(solution)/shard_map/all_gather | solution.py:54
  142.3 9.3 %fusion.34 = bf16[1024,2048]{1,0:T(8,128)(2,1)} fusion(bf16[1024,1024]{1,0:T(8,128)(2,1)} %all-gather.7.cloned.1.call-done, bf16[1024,2048]{1,0:T(8,128)(2,1)} %bitcast.88), kind=kOutput, calls=%fused_computation.74 | convolution fusion | flops 4294967296 | bytes 10485760 | tf_op jit(solution)/shard_map/dot_general | solution.py:53
  151.7 1.5 copy-done
  153.2 3.2 slice_reduce_fusion
  156.4 0.3 copy.20
  156.8 45.0 %reduce-scatter.6.cloned.1.call-done = bf16[128,2048]{1,0:T(8,128)(2,1)} async-done(((bf16[1024,2048]{1,0:T(8,128)(2,1)}), bf16[128,2048]{1,0:T(8,128)(2,1)}) %reduce-scatter.6.cloned.1.call-update) | async-done | bytes 524304 | tf_op jit(solution)/shard_map/reduce_scatter | solution.py:58
  201.7 1.9 subtract_convert_fusion
  204.0 5.6 %copy.24 = bf16[128,8,2,1024]{3,1,2,0:T(8,128)(2,1)} copy(bf16[128,8,2,1024]{3,2,1,0:T(2,128)(2,1)} %bitcast.83) | data formatting | bytes 8388608
  209.6 39.6 %all-gather.9.cloned.1.call-done = bf16[1024,2048]{1,0:T(8,128)(2,1)} async-done(((bf16[128,2048]{1,0:T(8,128)(2,1)}), bf16[1024,2048]{1,0:T(8,128)(2,1)}) %all-gather.9.cloned.1.call-update) | async-done | bytes 4194320 | tf_op jit(solution)/shard_map/all_gather | solution.py:61
  249.2 9.4 %fusion.35 = bf16[1024,1024]{1,0:T(8,128)(2,1)} fusion(bf16[1024,2048]{1,0:T(8,128)(2,1)} %all-gather.9.cloned.1.call-done, bf16[1024,2048]{1,0:T(8,128)(2,1)} %bitcast.87), kind=kOutput, calls=%fused_computation.75 | convolution fusion | flops 4294967296 | bytes 10485760 | tf_op jit(solution)/shard_map/dot_general | solution.py:47
  258.6 14.0 %all-gather = s32[8,1,2048]{2,1,0:T(1,128)S(1)} all-gather(s32[1,1,2048]{2,1,0:T(1,128)S(1)} %bitcast.94), channel_id=1, replica_groups=mesh['prow'=8,'pcol'=4] {'prow'}, dimensions={0}, use_global_device_ids=true | all-gather | bytes 73728 | tf_op jit(solution)/shard_map/all_gather | solution.py:29
  272.7 2.3 reduce-window.14
  275.0 0.3 slice_reduce_fusion.2
  275.6 5.7 %select_reduce_fusion = s32[8,256]{1,0:T(8,128)S(1)} fusion(s32[8,2048]{1,0:T(8,128)S(1)} %get-tuple-element.9, s32[8,2048]{1,0:T(8,128)S(1)} %get-tuple-element.10), kind=kLoop, calls=%fused_computation.2 | loop fusion | flops 12580864 | bytes 139264 | tf_op jit(solution)/shard_map/reduce_sum | solution.py:40
  281.4 11.3 %reduce-scatter.8.cloned.1.call-done = bf16[256,1024]{1,0:T(8,128)(2,1)} async-done(((bf16[1024,1024]{1,0:T(8,128)(2,1)}), bf16[256,1024]{1,0:T(8,128)(2,1)}) %reduce-scatter.8.cloned.1.call-update) | async-done | bytes 524304 | tf_op jit(solution)/shard_map/reduce_scatter | solution.py:63
  292.7 4.4 %fusion.3 = bf16[256,2048]{1,0:T(8,128)(2,1)S(1)} fusion(s32[2048]{0:T(1024)S(1)} %bitcast.99, bf16[256,1024]{1,0:T(8,128)(2,1)S(1)} %copy-done.1, bf16[256,1024]{1,0:T(8,128)(2,1)} %reduce-scatter.8.cloned.1.call-done), kind=kOutput, calls=%fused_computation.6 | convolution fusion | flops 2153775104 | bytes 2105344 | tf_op jit(solution)/shard_map/dot_general | solution.py:68
  297.1 1.0 copy.38
  298.2 4.6 %all-to-all-start = ((bf16[256,8,256]{2,0,1:T(8,128)(2,1)}), bf16[256,8,256]{2,0,1:T(8,128)(2,1)S(1)}, u32[]{:S(2)}, u32[]{:S(2)}) async-start(bf16[256,8,256]{2,0,1:T(8,128)(2,1)} %bitcast.80), calls=%async_computation.3 | async-start | bytes 2097152 | tf_op jit(solution)/shard_map/all_to_all | solution.py:69
  302.8 2.3 reduce-window.16
  305.7 23.6 %all-to-all-done = bf16[256,8,256]{2,0,1:T(8,128)(2,1)S(1)} async-done(((bf16[256,8,256]{2,0,1:T(8,128)(2,1)}), bf16[256,8,256]{2,0,1:T(8,128)(2,1)S(1)}, u32[]{:S(2)}, u32[]{:S(2)}) %all-to-all-start) | async-done | bytes 1048608 | tf_op jit(solution)/shard_map/all_to_all | solution.py:69
  329.4 0.6 copy.15
  330.0 0.5 reshape.153
  330.5 3.8 %fusion.6 = bf16[256,2,1,1024]{3,0,1,2:T(8,128)(2,1)S(1)} fusion(bf16[256,2048,1]{1,0,2:T(8,128)(2,1)S(1)} %reshape.153, s32[2,1024]{1,0:T(2,128)S(1)} %fusion.27), kind=kOutput, calls=%fused_computation.9 | convolution fusion | flops 2151677952 | bytes 2105344 | tf_op jit(solution)/shard_map/dot_general | solution.py:73
  334.3 2.0 copy.16
  (30 shorter events, 1.8 us)
Async XLA Ops:
  6.5 55.2 %all-gather.5.cloned.1.call-start = ((), (), s32[]{:S(2)}) async-start(), calls=%async_computation.4 | async-start | bytes 4718592 | tf_op jit(solution)/shard_map/all_gather | solution.py:50
  12.0 93.3 %reduce-scatter.4.cloned.1.call-start = ((), (), s32[]{:S(2)}) async-start(), calls=%async_computation.5 | async-start | bytes 2621440 | tf_op jit(solution)/shard_map/reduce_scatter | solution.py:52
  71.1 71.2 %all-gather.7.cloned.1.call-start = ((), (), s32[]{:S(2)}) async-start(), calls=%async_computation.6 | async-start | bytes 2621440 | tf_op jit(solution)/shard_map/all_gather | solution.py:54
  105.3 96.4 %reduce-scatter.6.cloned.1.call-start = ((), (), s32[]{:S(2)}) async-start(), calls=%async_computation.7 | async-start | bytes 4718592 | tf_op jit(solution)/shard_map/reduce_scatter | solution.py:58
  151.6 1.6 copy-start
  151.6 97.5 %all-gather.9.cloned.1.call-start = ((), (), s32[]{:S(2)}) async-start(), calls=%async_computation.8 | async-start | bytes 4718592 | tf_op jit(solution)/shard_map/all_gather | solution.py:61
  203.7 89.0 %reduce-scatter.8.cloned.1.call-start = ((), (), s32[]{:S(2)}) async-start(), calls=%async_computation.9 | async-start | bytes 2621440 | tf_op jit(solution)/shard_map/reduce_scatter | solution.py:63
  249.2 9.4 %copy-start.2 = (s32[2,1,1024]{2,1,0:T(1,128)S(1)}, s32[2,1,1024]{2,1,0:T(1,128)}, u32[]{:S(2)}) copy-start(s32[2,1,1024]{2,1,0:T(1,128)} %param.7) | copy-start | bytes 24580
  249.2 43.5 %copy-start.1 = (bf16[256,1024]{1,0:T(8,128)(2,1)S(1)}, bf16[256,1024]{1,0:T(8,128)(2,1)}, u32[]{:S(2)}) copy-start(bf16[256,1024]{1,0:T(8,128)(2,1)} %reduce-scatter.4.cloned.1.call-done) | copy-start | bytes 1572868
  298.2 31.2 %all-to-all-start = ((bf16[256,8,256]{2,0,1:T(8,128)(2,1)}), bf16[256,8,256]{2,0,1:T(8,128)(2,1)S(1)}, u32[]{:S(2)}, u32[]{:S(2)}) async-start(bf16[256,8,256]{2,0,1:T(8,128)(2,1)} %bitcast.80), calls=%async_computation.3 | async-start | bytes 2097152 | tf_op jit(solution)/shard_map/all_to_all | solution.py:69
Sparse Core Ops, SparseCore 0:
  12.1 49.5 all-gather.4
  71.2 33.9 reduce-scatter.3
  107.1 35.1 all-gather.6
  151.8 49.9 reduce-scatter.5
  203.8 45.3 all-gather.8
  258.7 33.9 reduce-scatter.7
where the time goes:
time: 344 us; the launch traced here: 343 us
  waiting for transfers between devices  223 us (65%)
  local copies, waits for them, and re-layouts  37.9 us (11%)
  matrix products  36.2 us (11%)
  blocking collectives  14 us (4%)
  between operations  13.6 us (4%)
  other arithmetic  13 us (4%)
  starting transfers between devices  5.24 us (2%)
    reduce_scatter x1, waiting for transfers between devices, body(): lax.psum_scatter(update_partial, 'prow', scatter_dimension=0, tiled=True)  45 us
    all_gather x1, waiting for transfers between devices, body(): lax.all_gather(lower_ready, 'prow', axis=0, tiled=True)  39.6 us
    all_gather x1, waiting for transfers between devices, body(): lax.all_gather(upper_rhs, 'prow', axis=0, tiled=True)  38.3 us
    reduce_scatter x1, waiting for transfers between devices, body(): lax.psum_scatter(first_partial, 'pcol', scatter_dimension=0, tiled=True)  34.1 us
    all_gather x1, waiting for transfers between devices, body(): lax.all_gather(upper_solved, 'pcol', axis=0, tiled=True)  31.2 us
    all_to_all x1, waiting for transfers between devices, body(): lax.all_to_all(chosen.reshape(own_cols, rows_axis, share), 'prow', split_...  23.6 us
    dot_general x2, matrix products, solve_with(): lax.dot_general(portion, inverse_mat, contract_last, preferred_element_ty...  18.7 us
    unnamed x12, local copies, waits for them, and re-layouts  17.4 us
  transfers between devices with their start and end apart: 7, of which 7 were waited for; matrix products, arithmetic and copies ran while one was open for 11% of the time, Pallas kernels for 0%

commit v1 on v0

--- a/solution.py
+++ b/solution.py
@@ -2,6 +2,27 @@
 import jax.numpy as jnp
 from jax import lax
 from jax.sharding import PartitionSpec as P
+
+
+def joined_along(blocks, dim):
+    lengths = list(blocks.shape[1:])
+    lengths[dim] *= blocks.shape[0]
+    return jnp.moveaxis(blocks, 0, dim).reshape(lengths)
+
+
+def collected_by_bits(x, axis):
+    devices, mine = (lax.axis_size(axis), lax.axis_index(axis))
+    blocks, stride = (x[None], 1)
+    while stride < devices:
+        other = lax.ppermute(blocks, axis, [(i, i ^ stride) for i in range(devices)])
+        low = mine & stride == 0
+        blocks = jnp.concatenate([jnp.where(low, blocks, other), jnp.where(low, other, blocks)])
+        stride *= 2
+    return blocks
+
+
+def doubled_up(array, axis, dim):
+    return joined_along(collected_by_bits(array, axis), dim)
 
 
 def body(right_side, inverse_blocks, coupling, pivots):
@@ -51,9 +72,7 @@
     )
     upper_solved = lax.psum_scatter(first_partial, "pcol", scatter_dimension=0, tiled=True)
     update_partial = jnp.dot(
-        lax.all_gather(upper_solved, "pcol", axis=0, tiled=True),
-        coupling_mat,
-        preferred_element_type=bf16,
+        doubled_up(upper_solved, "pcol", 0), coupling_mat, preferred_element_type=bf16
     )
     update = lax.psum_scatter(update_partial, "prow", scatter_dimension=0, tiled=True)
     lower_ready = (lower_rhs - update.astype(f32)).astype(bf16)

time: 344 us -> 342 us (level)
    all_gather x1 -> x0, waiting for transfers between devices: 31.2 us -> none  [body(): lax.all_gather(upper_solved, 'pcol', axis=0, tiled=True)]
    ppermute x0 -> x2, waiting for transfers between devices: none -> 31 us  [collected_by_bits(): lax.ppermute(blocks, axis, [(i, i ^ stride) for i in range(devices)])]
  transfers between devices with their start and end apart: 7 -> 8, of which waited for: 7 -> 8; matrix products, arithmetic and copies ran while one was open for 11% -> 10% of each run, Pallas kernels for 0% -> 0%
where the time goes in v1:
time: 342 us
  waiting for transfers between devices  223 us (65%)
  local copies, waits for them, and re-layouts  35.9 us (10%)
  matrix products  33.1 us (10%)
  other arithmetic  14.5 us (4%)
  blocking collectives  14 us (4%)
  between operations  13.3 us (4%)
  starting transfers between devices  8.18 us (2%)
    reduce_scatter x1, waiting for transfers between devices, body(): lax.psum_scatter(update_partial, 'prow', scatter_dimension=0, tiled=True)  44.9 us
    all_gather x1, waiting for transfers between devices, body(): lax.all_gather(lower_ready, 'prow', axis=0, tiled=True)  39.6 us
    all_gather x1, waiting for transfers between devices, body(): lax.all_gather(upper_rhs, 'prow', axis=0, tiled=True)  38.3 us
    reduce_scatter x1, waiting for transfers between devices, body(): lax.psum_scatter(first_partial, 'pcol', scatter_dimension=0, tiled=True)  33.9 us
    ppermute x2, waiting for transfers between devices, collected_by_bits(): lax.ppermute(blocks, axis, [(i, i ^ stride) for i in range(devices)])  31 us
    all_to_all x1, waiting for transfers between devices, body(): lax.all_to_all(chosen.reshape(own_cols, rows_axis, share), 'prow', split_...  23.6 us
    dot_general x2, matrix products, solve_with(): lax.dot_general(portion, inverse_mat, contract_last, preferred_element_ty...  18.7 us
    unnamed x12, local copies, waits for them, and re-layouts  15.4 us
  transfers between devices with their start and end apart: 8, of which 8 were waited for; matrix products, arithmetic and copies ran while one was open for 10% of the time, Pallas kernels for 0%

profile of v1, /device:TPU:0, one launch (start us, length us, event | category | flops | bytes accessed | tf_op | source)
XLA Modules:
  0.0 341.9 jit_solution(6951894816708713767)
XLA Ops:
  6.5 4.5 %fusion.9 = bf16[128,2,1024]{2,1,0:T(2,128)(2,1)S(1)} fusion(f32[128,4,1,1024]{3,2,1,0:T(1,128)} %param.4), kind=kLoop, calls=%fused_computation.13 | loop fusion | bytes 1048576 | tf_op jit(solution)/shard_map/slice | solution.py:46
  11.0 0.9 copy.21
  12.0 8.0 %fusion.32 = (bf16[1,1,1,1024,2,1,1024]{6,4,5,3,2,1,0:T(2,128)(2,1)}, bf16[1,1,1,1024,2,1,1024]{6,4,5,3,2,1,0:T(2,128)(2,1)S(1)}) fusion(bf16[2,1,1,1024,2,1,1024]{6,4,5,3,2,1,0:T(2,128)(2,1)} %param.5), kind=kLoop, calls=%fused_computation.78 | loop fusion | bytes 16777216 | tf_op jit(solution)/shard_map/slice | solution.py:80
  20.0 3.4 copy.22
  23.4 38.3 %all-gather.4.cloned.1.call-done = bf16[1024,2048]{1,0:T(8,128)(2,1)} async-done(((bf16[128,2048]{1,0:T(8,128)(2,1)}), bf16[1024,2048]{1,0:T(8,128)(2,1)}) %all-gather.4.cloned.1.call-update) | async-done | bytes 4194320 | tf_op jit(solution)/shard_map/all_gather | solution.py:71
  61.7 9.4 %fusion.33 = bf16[1024,1024]{1,0:T(8,128)(2,1)} fusion(bf16[1024,2048]{1,0:T(8,128)(2,1)} %all-gather.4.cloned.1.call-done, bf16[1024,2048]{1,0:T(8,128)(2,1)} %bitcast.91), kind=kOutput, calls=%fused_computation.79 | convolution fusion | flops 4294967296 | bytes 10485760 | tf_op jit(solution)/shard_map/dot_general | solution.py:68
  71.3 33.9 %reduce-scatter.4.cloned.1.call-done = bf16[256,1024]{1,0:T(8,128)(2,1)} async-done(((bf16[1024,1024]{1,0:T(8,128)(2,1)}), bf16[256,1024]{1,0:T(8,128)(2,1)}) %reduce-scatter.4.cloned.1.call-update) | async-done | bytes 524304 | tf_op jit(solution)/shard_map/reduce_scatter | solution.py:73
  105.3 1.5 collective-permute-start
  106.7 12.2 %collective-permute-done = bf16[1,256,1024]{2,1,0:T(8,128)(2,1)S(1)} collective-permute-done((bf16[1,256,1024]{2,1,0:T(8,128)(2,1)}, bf16[1,256,1024]{2,1,0:T(8,128)(2,1)S(1)}, u32[]{:S(2)}, u32[]{:S(2)}) %collective-permute-start) | collective-permute-done | bytes 524320 | tf_op jit(solution)/shard_map/ppermute | solution.py:17
  119.0 1.1 broadcast_select_fusion.3
  120.2 1.5 collective-permute-start.1
  121.7 3.6 %copy.23 = bf16[128,8,2,1024]{3,1,2,0:T(8,128)(2,1)S(1)} copy(bf16[128,8,2,1024]{3,2,1,0:T(2,128)(2,1)} %bitcast.89) | data formatting | bytes 8388608
  125.4 18.8 %collective-permute-done.1 = bf16[2,256,1024]{2,1,0:T(8,128)(2,1)S(1)} collective-permute-done((bf16[2,256,1024]{2,1,0:T(8,128)(2,1)S(1)}, bf16[2,256,1024]{2,1,0:T(8,128)(2,1)S(1)}, u32[]{:S(2)}, u32[]{:S(2)}) %collective-permute-start.1) | collective-permute-done | bytes 1048608 | tf_op jit(solution)/shard_map/ppermute | solution.py:17
  144.5 6.2 %fusion.34 = bf16[1024,2048]{1,0:T(8,128)(2,1)} fusion(bf16[1024,1024]{1,0:T(8,128)(2,1)S(1)} %bitcast.96, bf16[1024,2048]{1,0:T(8,128)(2,1)S(1)} %bitcast.90), kind=kOutput, calls=%fused_computation.80 | convolution fusion | flops 4294967296 | bytes 10485760 | tf_op jit(solution)/shard_map/dot_general | solution.py:74
  150.7 1.5 copy-done
  152.2 3.2 slice_reduce_fusion
  155.8 44.9 %reduce-scatter.6.cloned.1.call-done = bf16[128,2048]{1,0:T(8,128)(2,1)} async-done(((bf16[1024,2048]{1,0:T(8,128)(2,1)}), bf16[128,2048]{1,0:T(8,128)(2,1)}) %reduce-scatter.6.cloned.1.call-update) | async-done | bytes 524304 | tf_op jit(solution)/shard_map/reduce_scatter | solution.py:77
  200.7 1.9 subtract_convert_fusion
  203.0 5.6 %copy.24 = bf16[128,8,2,1024]{3,1,2,0:T(8,128)(2,1)} copy(bf16[128,8,2,1024]{3,2,1,0:T(2,128)(2,1)} %bitcast.87) | data formatting | bytes 8388608
  208.6 39.6 %all-gather.6.cloned.1.call-done = bf16[1024,2048]{1,0:T(8,128)(2,1)} async-done(((bf16[128,2048]{1,0:T(8,128)(2,1)}), bf16[1024,2048]{1,0:T(8,128)(2,1)}) %all-gather.6.cloned.1.call-update) | async-done | bytes 4194320 | tf_op jit(solution)/shard_map/all_gather | solution.py:80
  248.2 9.4 %fusion.35 = bf16[1024,1024]{1,0:T(8,128)(2,1)} fusion(bf16[1024,2048]{1,0:T(8,128)(2,1)} %all-gather.6.cloned.1.call-done, bf16[1024,2048]{1,0:T(8,128)(2,1)} %bitcast.92), kind=kOutput, calls=%fused_computation.81 | convolution fusion | flops 4294967296 | bytes 10485760 | tf_op jit(solution)/shard_map/dot_general | solution.py:68
  257.6 14.0 %all-gather = s32[8,1,2048]{2,1,0:T(1,128)S(1)} all-gather(s32[1,1,2048]{2,1,0:T(1,128)S(1)} %bitcast.100), channel_id=1, replica_groups=mesh['prow'=8,'pcol'=4] {'prow'}, dimensions={0}, use_global_device_ids=true | all-gather | bytes 73728 | tf_op jit(solution)/shard_map/all_gather | solution.py:50
  271.7 2.3 reduce-window.14
  274.6 5.7 %select_reduce_fusion = s32[8,256]{1,0:T(8,128)S(1)} fusion(s32[8,2048]{1,0:T(8,128)S(1)} %get-tuple-element.13, s32[8,2048]{1,0:T(8,128)S(1)} %get-tuple-element.14), kind=kLoop, calls=%fused_computation.2 | loop fusion | flops 12580864 | bytes 139264 | tf_op jit(solution)/shard_map/reduce_sum | solution.py:61
  280.4 11.3 %reduce-scatter.8.cloned.1.call-done = bf16[256,1024]{1,0:T(8,128)(2,1)} async-done(((bf16[1024,1024]{1,0:T(8,128)(2,1)}), bf16[256,1024]{1,0:T(8,128)(2,1)}) %reduce-scatter.8.cloned.1.call-update) | async-done | bytes 524304 | tf_op jit(solution)/shard_map/reduce_scatter | solution.py:82
  291.7 4.4 %fusion.3 = bf16[256,2048]{1,0:T(8,128)(2,1)S(1)} fusion(s32[2048]{0:T(1024)S(1)} %bitcast.105, bf16[256,1024]{1,0:T(8,128)(2,1)S(1)} %copy-done.1, bf16[256,1024]{1,0:T(8,128)(2,1)} %reduce-scatter.8.cloned.1.call-done), kind=kOutput, calls=%fused_computation.6 | convolution fusion | flops 2153775104 | bytes 2105344 | tf_op jit(solution)/shard_map/dot_general | solution.py:87
  296.1 1.0 copy.38
  297.2 4.6 %all-to-all-start = ((bf16[256,8,256]{2,0,1:T(8,128)(2,1)}), bf16[256,8,256]{2,0,1:T(8,128)(2,1)S(1)}, u32[]{:S(2)}, u32[]{:S(2)}) async-start(bf16[256,8,256]{2,0,1:T(8,128)(2,1)} %bitcast.84), calls=%async_computation.3 | async-start | bytes 2097152 | tf_op jit(solution)/shard_map/all_to_all | solution.py:88
  301.8 2.3 reduce-window.16
  304.7 23.6 %all-to-all-done = bf16[256,8,256]{2,0,1:T(8,128)(2,1)S(1)} async-done(((bf16[256,8,256]{2,0,1:T(8,128)(2,1)}), bf16[256,8,256]{2,0,1:T(8,128)(2,1)S(1)}, u32[]{:S(2)}, u32[]{:S(2)}) %all-to-all-start) | async-done | bytes 1048608 | tf_op jit(solution)/shard_map/all_to_all | solution.py:88
  329.5 3.8 %fusion.6 = bf16[256,2,1,1024]{3,0,1,2:T(8,128)(2,1)S(1)} fusion(bf16[256,2048,1]{1,0,2:T(8,128)(2,1)S(1)} %reshape.157, s32[2,1024]{1,0:T(2,128)S(1)} %fusion.27), kind=kOutput, calls=%fused_computation.10 | convolution fusion | flops 2151677952 | bytes 2105344 | tf_op jit(solution)/shard_map/dot_general | solution.py:92
  333.3 2.0 copy.16
  (35 shorter events, 3.9 us)
Async XLA Ops:
  6.5 55.2 %all-gather.4.cloned.1.call-start = ((), (), s32[]{:S(2)}) async-start(), calls=%async_computation.4 | async-start | bytes 4718592 | tf_op jit(solution)/shard_map/all_gather | solution.py:71
  12.0 93.3 %reduce-scatter.4.cloned.1.call-start = ((), (), s32[]{:S(2)}) async-start(), calls=%async_computation.5 | async-start | bytes 2621440 | tf_op jit(solution)/shard_map/reduce_scatter | solution.py:73
  71.1 129.6 %reduce-scatter.6.cloned.1.call-start = ((), (), s32[]{:S(2)}) async-start(), calls=%async_computation.6 | async-start | bytes 4718592 | tf_op jit(solution)/shard_map/reduce_scatter | solution.py:77
  105.3 13.7 %collective-permute-start = (bf16[1,256,1024]{2,1,0:T(8,128)(2,1)}, bf16[1,256,1024]{2,1,0:T(8,128)(2,1)S(1)}, u32[]{:S(2)}, u32[]{:S(2)}) collective-permute-start(bf16[1,256,1024]{2,1,0:T(8,128)(2,1)} %bitcast.99), channel_id=1, source_target_pairs={{0,1},{1,0},{2,3},{3,2},{4,5},{5,4},{6,7},{7,6},{8,9},{9,8},{10,11... | collective-permute-start | bytes 1572872 | tf_op jit(solution)/shard_map/ppermute | solution.py:17
  120.2 23.9 %collective-permute-start.1 = (bf16[2,256,1024]{2,1,0:T(8,128)(2,1)S(1)}, bf16[2,256,1024]{2,1,0:T(8,128)(2,1)S(1)}, u32[]{:S(2)}, u32[]{:S(2)}) collective-permute-start(bf16[2,256,1024]{2,1,0:T(8,128)(2,1)S(1)} %pad_maximum_fusion.1), channel_id=1, source_target_pairs={{0,2},{1,3},{2,0},{3,1},{4,6},{5,7},{6,4},{7,5},{8,10},{9,11},{10,... | collective-permute-start | bytes 3145736 | tf_op jit(solution)/shard_map/ppermute | solution.py:17
  150.6 1.6 copy-start
  150.7 97.5 %all-gather.6.cloned.1.call-start = ((), (), s32[]{:S(2)}) async-start(), calls=%async_computation.7 | async-start | bytes 4718592 | tf_op jit(solution)/shard_map/all_gather | solution.py:80
  202.7 89.0 %reduce-scatter.8.cloned.1.call-start = ((), (), s32[]{:S(2)}) async-start(), calls=%async_computation.8 | async-start | bytes 2621440 | tf_op jit(solution)/shard_map/reduce_scatter | solution.py:82
  248.2 9.4 %copy-start.2 = (s32[2,1,1024]{2,1,0:T(1,128)S(1)}, s32[2,1,1024]{2,1,0:T(1,128)}, u32[]{:S(2)}) copy-start(s32[2,1,1024]{2,1,0:T(1,128)} %param.7) | copy-start | bytes 24580
  248.2 43.5 %copy-start.1 = (bf16[256,1024]{1,0:T(8,128)(2,1)S(1)}, bf16[256,1024]{1,0:T(8,128)(2,1)}, u32[]{:S(2)}) copy-start(bf16[256,1024]{1,0:T(8,128)(2,1)} %reduce-scatter.4.cloned.1.call-done) | copy-start | bytes 1572868
  297.2 31.2 %all-to-all-start = ((bf16[256,8,256]{2,0,1:T(8,128)(2,1)}), bf16[256,8,256]{2,0,1:T(8,128)(2,1)S(1)}, u32[]{:S(2)}, u32[]{:S(2)}) async-start(bf16[256,8,256]{2,0,1:T(8,128)(2,1)} %bitcast.84), calls=%async_computation.3 | async-start | bytes 2097152 | tf_op jit(solution)/shard_map/all_to_all | solution.py:88
Sparse Core Ops, SparseCore 0:
  12.1 49.5 all-gather.3
  71.2 33.9 reduce-scatter.3
  150.8 49.8 reduce-scatter.5
  202.8 45.3 all-gather.5
  257.7 33.9 reduce-scatter.7
